TPU v7x, 32 devices: a whole 2x2x4 slice. The times are simulated.
32 devices in a mesh: grp: 2 (over y), src: 8 (over z, x), tgt: 2 (over core).
Axes of the slice: x: 2, y: 2, z: 4, core: 2. Of those that a mesh axis runs over, the one named last changes fastest.
Arguments:
- source_feat: float32 [256, 64, 128], P(('grp', 'src')), parts along dimension 0, may hold values from -1.2 to 1.2
- target_feat: float32 [32, 64, 128], P(('grp', 'src', 'tgt')), parts along dimension 0, may hold values from -1.2 to 1.2
- log_mass_src: float32 [256, 128], P(('grp', 'src')), parts along dimension 0, may hold values from -3 to 3
- log_mass_tgt: float32 [32, 128], P(('grp', 'src', 'tgt')), parts along dimension 0, may hold values from -3 to 3
- potential_tgt: float32 [32, 128], P(('grp', 'src', 'tgt')), parts along dimension 0, may hold values from -6 to 152
- support: int32 [256, 2, 8], P(('grp', 'src'), 'tgt'), parts along dimension 0, may hold values from 0 to 7, as said below
- counts: int32 [256, 2], P(('grp', 'src'), 'tgt'), parts along dimension 0, may hold values from 1 to 8, as said below
Outputs:
- potential_src: float32 [256, 128], P(('grp', 'src')), parts along dimension 0
- potential_new: float32 [32, 128], P(('grp', 'src', 'tgt')), parts along dimension 0
There are 2 independent parts, one for each index of `grp`. A program takes and returns all parts, laid end to end along the dimension named above; each array names one. Nothing has to cross between parts.
Inputs may be any that keep to these rules, and one draw needn't show every extreme that they name: `support`: within one list the first counts entries are distinct; unused entries are also valid indices and are ignored; every target block of a shard is named within the used entries of some source block row. `counts`: the source block rows of one index of src share a load level, so some devices use far more slots than others; some list is full in every draw.
All inputs are finite; a program needn't handle non-finite values.
Results may differ from a plain program's by a relative error of at most 0.000096.
Values sent between devices are 32-bit elements; how exact they have to be, the bound alone decides.
A program may use at most 64 MiB of HBM per device.

v0:
```python
import math
import jax
import jax.numpy as jnp
from jax import lax
from jax.sharding import PartitionSpec as P

entropic = 0.5
very_low = -1e30


def merged(part, axis, combine):
    gathered = jax.tree.map(lambda a: lax.all_gather(a, axis), part)

    def take(source):
        return jax.tree.map(lambda a: lax.dynamic_index_in_dim(a, source, 0, False), gathered)

    return lax.fori_loop(
        1, lax.axis_size(axis), lambda source, state: combine(state, take(source)), take(0)
    )


def cost_tiles(source_blk, source_sq, target_blk, target_sq):
    cross = jnp.einsum(
        "...fi,...fj->...ij", source_blk, target_blk, precision=lax.Precision.HIGHEST
    )
    return source_sq[..., :, None] + target_sq[..., None, :] - 2.0 * cross


def row_stats(cost, mass_tgt, poten_tgt, usable):
    scores = mass_tgt[..., None, :] + (poten_tgt[..., None, :] - cost) / entropic
    scores = jnp.where(usable[..., None, None], scores, very_low)
    peak = jnp.max(scores, axis=(1, 3))
    total = jnp.sum(jnp.exp(scores - peak[:, None, :, None]), axis=(1, 3))
    return (peak, total)


def column_stats(cost, mass_src, poten_src, usable):
    scores = mass_src[:, None, :, None] + (poten_src[:, None, :, None] - cost) / entropic
    peak = jnp.max(scores, axis=2)
    total = jnp.sum(jnp.exp(scores - peak[:, :, None, :]), axis=2)
    peak = jnp.where(usable[..., None], peak, very_low)
    total = jnp.where(usable[..., None], total, 0.0)
    return (peak, total)


def merge_pair(first_pair, second_pair):
    first_peak, first_total = first_pair
    second_peak, second_total = second_pair
    highest = jnp.maximum(first_peak, second_peak)
    summed = first_total * jnp.exp(first_peak - highest) + second_total * jnp.exp(
        second_peak - highest
    )
    return (highest, summed)


def segment_merge(peaks, totals, seg_ids, segments):
    best = jax.ops.segment_max(peaks, seg_ids, num_segments=segments + 1)
    best = jnp.maximum(best, very_low)
    summed = jax.ops.segment_sum(
        totals * jnp.exp(peaks - best[seg_ids]), seg_ids, num_segments=segments + 1
    )
    return (best[:segments], summed[:segments])


def per_device(
    source_feat, target_feat, log_mass_src, log_mass_tgt, potential_tgt, support, counts
):
    target_all, mass_all, poten_all = (
        lax.all_gather(target_feat, "src", axis=0, tiled=True),
        lax.all_gather(log_mass_tgt, "src", axis=0, tiled=True),
        lax.all_gather(potential_tgt, "src", axis=0, tiled=True),
    )
    blocks = target_all.shape[0]
    rows_here = source_feat.shape[0]
    slots_here = support.shape[2]
    cells = source_feat.shape[2]
    indices = support[:, 0, :]
    limits = counts[:, 0]
    usable = jnp.arange(slots_here, dtype=jnp.int32)[None, :] < limits[:, None]
    source_sq = jnp.sum(source_feat * source_feat, axis=1)
    target_sq = jnp.sum(target_all * target_all, axis=1)
    width = math.gcd(rows_here, 4)

    def grouped(array):
        return array.reshape((rows_here // width, width) + array.shape[1:])

    def row_pass(items):
        source_blk, source_nrm, ids_here, use_here = items
        cost = cost_tiles(
            source_blk[:, None], source_nrm[:, None], target_all[ids_here], target_sq[ids_here]
        )
        return row_stats(cost, mass_all[ids_here], poten_all[ids_here], use_here)

    peak, total = lax.map(
        row_pass, (grouped(source_feat), grouped(source_sq), grouped(indices), grouped(usable))
    )
    peak = peak.reshape(rows_here, cells)
    total = total.reshape(rows_here, cells)
    peak_all, total_all = merged((peak, total), "tgt", merge_pair)
    potential_src = -entropic * (peak_all + jnp.log(total_all))

    def column_pass(items):
        source_blk, source_nrm, mass_here, poten_here, ids_here, use_here = items
        cost = cost_tiles(
            source_blk[:, None], source_nrm[:, None], target_all[ids_here], target_sq[ids_here]
        )
        return column_stats(cost, mass_here, poten_here, use_here)

    peaks, totals = lax.map(
        column_pass,
        (
            grouped(source_feat),
            grouped(source_sq),
            grouped(log_mass_src),
            grouped(potential_src),
            grouped(indices),
            grouped(usable),
        ),
    )
    seg_ids = jnp.where(usable, indices, blocks).reshape(-1)
    best, summed = segment_merge(
        peaks.reshape(-1, cells), totals.reshape(-1, cells), seg_ids, blocks
    )
    share = blocks // lax.axis_size("src")
    own_start = lax.axis_index("src") * share
    highest = lax.pmax(best, "src")
    whole = lax.psum(summed * jnp.exp(best - highest), "src")
    own_peak = lax.dynamic_slice_in_dim(highest, own_start, share, 0)
    own_total = lax.dynamic_slice_in_dim(whole, own_start, share, 0)
    potential_new = -entropic * (own_peak + jnp.log(own_total))
    return (potential_src, potential_new)


def solution(mesh):
    in_specs = (
        P(("grp", "src"), None, None),
        P(("grp", "src", "tgt"), None, None),
        P(("grp", "src"), None),
        P(("grp", "src", "tgt"), None),
        P(("grp", "src", "tgt"), None),
        P(("grp", "src"), "tgt", None),
        P(("grp", "src"), "tgt"),
    )
    out_specs = (P(("grp", "src"), None), P(("grp", "src", "tgt"), None))
    return jax.shard_map(
        per_device, mesh=mesh, in_specs=in_specs, out_specs=out_specs, check_vma=False
    )
```

profile of v0, /device:TPU:0, one launch (start us, length us, event | category | flops | bytes accessed | tf_op | source)
XLA Modules:
  0.0 177.5 jit_solution(18147925197401593971)
XLA Ops:
  1.2 1.3 reduce.3
  2.6 0.8 copy.19
  3.4 22.4 %all-gather = f32[8,1,128]{2,1,0:T(1,128)S(1)} all-gather(f32[1,1,128]{2,1,0:T(1,128)} %bitcast.189), channel_id=1, replica_groups=mesh['grp'=2,'src'=8,'tgt'=2] {'src'}, dimensions={0}, use_global_device_ids=true | all-gather | bytes 4608 | tf_op jit(solution)/shard_map/all_gather | solution.py:70
  25.8 16.5 %all-gather.1 = f32[8,1,128]{2,1,0:T(1,128)S(1)} all-gather(f32[1,1,128]{2,1,0:T(1,128)} %bitcast.190), channel_id=1, replica_groups=mesh['grp'=2,'src'=8,'tgt'=2] {'src'}, dimensions={0}, use_global_device_ids=true | all-gather | bytes 4608 | tf_op jit(solution)/shard_map/all_gather | solution.py:71
  42.3 1.1 multiply_reduce_fusion
  43.4 31.0 %all_gather.17 = f32[8,64,128]{2,1,0:T(8,128)S(1)} all-gather(f32[1,64,128]{2,1,0:T(8,128)} %param.12), channel_id=1, replica_groups=mesh['grp'=2,'src'=8,'tgt'=2] {'src'}, dimensions={0}, use_global_device_ids=true | all-gather | bytes 294912 | tf_op jit(solution)/shard_map/all_gather | solution.py:69
  74.5 35.7 %while.8 = (s32[]{:T(128)}, f32[4,4,128]{2,1,0:T(4,128)S(1)}, f32[4,4,128]{2,1,0:T(4,128)S(1)}, pred[4,4,8]{2,1,0:T(4,128)(4,1)S(1)}, s32[4,4,8]{2,1,0:T(4,128)S...) while((s32[]{:T(128)}, f32[4,4,128]{2,1,0:T(4,128)S(1)}, ...), condition=%wide.region_5.6_spmd, body=%wide.region_2.5_spmd.sunk | while | flops 407896160 | bytes 7644529 | solution.py:94
  74.6 0.6 gather_fusion
  75.2 0.6 gather_fusion.1
  75.8 0.6 gather_fusion.2
  77.0 6.1 %fusion.44 = (f32[4,128]{1,0:T(4,128)S(1)}, f32[4,8,128,128]{2,3,1,0:T(8,128)S(1)}) fusion(f32[4,8,64,128]{3,2,1,0:T(8,128)S(1)} %bitcast.172, f32[4,4,64,128]{3,2,1,0:T(8,128)} %get-tuple-element.388, s32[]{:T(128)S(6)} %copy.30, f32[4,8,128]{2,1,0:T(8,128)S(1)} %bitcast.175, f32[4,128]{1,0:T(4,128)S(1)} %dynamic-slice_bitcast_fusion.9, ...), kind=kOutput, calls=%fused_computation.75.clone.1 | convolution fusion | flops 406846976 | bytes 3330084 | tf_op jit(solution)/shard_map/while/body/eval_jaxpr/...fi,...fj->...ij/dot_general | solution.py:23
  83.5 0.6 gather_fusion
  84.2 0.6 gather_fusion.1
  84.7 0.6 gather_fusion.2
  85.9 6.1 %fusion.44 = (f32[4,128]{1,0:T(4,128)S(1)}, f32[4,8,128,128]{2,3,1,0:T(8,128)S(1)}) fusion(f32[4,8,64,128]{3,2,1,0:T(8,128)S(1)} %bitcast.172, f32[4,4,64,128]{3,2,1,0:T(8,128)} %get-tuple-element.388, s32[]{:T(128)S(6)} %copy.30, f32[4,8,128]{2,1,0:T(8,128)S(1)} %bitcast.175, f32[4,128]{1,0:T(4,128)S(1)} %dynamic-slice_bitcast_fusion.9, ...), kind=kOutput, calls=%fused_computation.75.clone.1 | convolution fusion | flops 406846976 | bytes 3330084 | tf_op jit(solution)/shard_map/while/body/eval_jaxpr/...fi,...fj->...ij/dot_general | solution.py:23
  92.5 0.6 gather_fusion
  93.1 0.6 gather_fusion.1
  93.7 0.6 gather_fusion.2
  94.8 6.1 %fusion.44 = (f32[4,128]{1,0:T(4,128)S(1)}, f32[4,8,128,128]{2,3,1,0:T(8,128)S(1)}) fusion(f32[4,8,64,128]{3,2,1,0:T(8,128)S(1)} %bitcast.172, f32[4,4,64,128]{3,2,1,0:T(8,128)} %get-tuple-element.388, s32[]{:T(128)S(6)} %copy.30, f32[4,8,128]{2,1,0:T(8,128)S(1)} %bitcast.175, f32[4,128]{1,0:T(4,128)S(1)} %dynamic-slice_bitcast_fusion.9, ...), kind=kOutput, calls=%fused_computation.75.clone.1 | convolution fusion | flops 406846976 | bytes 3330084 | tf_op jit(solution)/shard_map/while/body/eval_jaxpr/...fi,...fj->...ij/dot_general | solution.py:23
  101.4 0.6 gather_fusion
  102.0 0.6 gather_fusion.1
  102.6 0.6 gather_fusion.2
  103.8 6.1 %fusion.44 = (f32[4,128]{1,0:T(4,128)S(1)}, f32[4,8,128,128]{2,3,1,0:T(8,128)S(1)}) fusion(f32[4,8,64,128]{3,2,1,0:T(8,128)S(1)} %bitcast.172, f32[4,4,64,128]{3,2,1,0:T(8,128)} %get-tuple-element.388, s32[]{:T(128)S(6)} %copy.30, f32[4,8,128]{2,1,0:T(8,128)S(1)} %bitcast.175, f32[4,128]{1,0:T(4,128)S(1)} %dynamic-slice_bitcast_fusion.9, ...), kind=kOutput, calls=%fused_computation.75.clone.1 | convolution fusion | flops 406846976 | bytes 3330084 | tf_op jit(solution)/shard_map/while/body/eval_jaxpr/...fi,...fj->...ij/dot_general | solution.py:23
  110.2 1.8 %all_gather.19 = f32[2,16,128]{2,1,0:T(8,128)S(1)} all-gather(f32[1,16,128]{2,1,0:T(8,128)S(1)} %bitcast.188), channel_id=1, replica_groups=mesh['grp'=2,'src'=8,'tgt'=2] {'tgt'}, dimensions={0}, use_global_device_ids=true | all-gather | bytes 24576 | tf_op jit(solution)/shard_map/all_gather | solution.py:12
  112.0 1.8 %all_gather.18 = f32[2,16,128]{2,1,0:T(8,128)S(1)} all-gather(f32[1,16,128]{2,1,0:T(8,128)S(1)} %bitcast.187), channel_id=1, replica_groups=mesh['grp'=2,'src'=8,'tgt'=2] {'tgt'}, dimensions={0}, use_global_device_ids=true | all-gather | bytes 24576 | tf_op jit(solution)/shard_map/all_gather | solution.py:12
  113.9 0.6 fusion.19
  114.8 22.8 %while.9 = (s32[]{:T(128)}, f32[4,4,8,128]{3,2,1,0:T(8,128)S(1)}, f32[4,4,8,128]{3,2,1,0:T(8,128)S(1)}, pred[4,4,8]{2,1,0:T(4,128)(4,1)S(1)}, f32[4,4,128]{2,1,0...) while((s32[]{:T(128)}, f32[4,4,8,128]{3,2,1,0:T(8,128)S(1)}, ...), condition=%wide.region_9.10_spmd, body=%wide.region_6.9_spmd.sunk | while | flops 407372896 | bytes 7659093 | solution.py:109
  114.9 0.6 gather_fusion.4
  115.6 0.6 gather_fusion.5
  116.2 0.7 dynamic-slice_bitcast_fusion.12
  116.9 3.2 %fusion.46 = (f32[4,8,128]{2,1,0:T(8,128)S(1)}, f32[4,8,128,128]{3,2,1,0:T(8,128)S(1)}) fusion(f32[4,8,64,128]{3,2,1,0:T(8,128)S(1)} %bitcast.171, f32[4,4,64,128]{3,2,1,0:T(8,128)} %get-tuple-element.424, s32[]{:T(128)S(6)} %copy.39, f32[4,8,128]{2,1,0:T(8,128)S(1)} %bitcast.174, f32[4,128]{1,0:T(4,128)S(1)} %get-tuple-element.348, ...), kind=kOutput, calls=%fused_computation.76.clone.1 | convolution fusion | flops 406319104 | bytes 3315716 | tf_op jit(solution)/shard_map/while/body/eval_jaxpr/...fi,...fj->...ij/dot_general | solution.py:23
  120.6 0.6 gather_fusion.4
  121.3 0.6 gather_fusion.5
  121.9 0.7 dynamic-slice_bitcast_fusion.12
  122.5 3.2 %fusion.46 = (f32[4,8,128]{2,1,0:T(8,128)S(1)}, f32[4,8,128,128]{3,2,1,0:T(8,128)S(1)}) fusion(f32[4,8,64,128]{3,2,1,0:T(8,128)S(1)} %bitcast.171, f32[4,4,64,128]{3,2,1,0:T(8,128)} %get-tuple-element.424, s32[]{:T(128)S(6)} %copy.39, f32[4,8,128]{2,1,0:T(8,128)S(1)} %bitcast.174, f32[4,128]{1,0:T(4,128)S(1)} %get-tuple-element.348, ...), kind=kOutput, calls=%fused_computation.76.clone.1 | convolution fusion | flops 406319104 | bytes 3315716 | tf_op jit(solution)/shard_map/while/body/eval_jaxpr/...fi,...fj->...ij/dot_general | solution.py:23
  126.3 0.6 gather_fusion.4
  127.0 0.6 gather_fusion.5
  127.6 0.7 dynamic-slice_bitcast_fusion.12
  128.2 3.2 %fusion.46 = (f32[4,8,128]{2,1,0:T(8,128)S(1)}, f32[4,8,128,128]{3,2,1,0:T(8,128)S(1)}) fusion(f32[4,8,64,128]{3,2,1,0:T(8,128)S(1)} %bitcast.171, f32[4,4,64,128]{3,2,1,0:T(8,128)} %get-tuple-element.424, s32[]{:T(128)S(6)} %copy.39, f32[4,8,128]{2,1,0:T(8,128)S(1)} %bitcast.174, f32[4,128]{1,0:T(4,128)S(1)} %get-tuple-element.348, ...), kind=kOutput, calls=%fused_computation.76.clone.1 | convolution fusion | flops 406319104 | bytes 3315716 | tf_op jit(solution)/shard_map/while/body/eval_jaxpr/...fi,...fj->...ij/dot_general | solution.py:23
  132.0 0.6 gather_fusion.4
  132.7 0.6 gather_fusion.5
  133.3 0.7 dynamic-slice_bitcast_fusion.12
  133.9 3.2 %fusion.46 = (f32[4,8,128]{2,1,0:T(8,128)S(1)}, f32[4,8,128,128]{3,2,1,0:T(8,128)S(1)}) fusion(f32[4,8,64,128]{3,2,1,0:T(8,128)S(1)} %bitcast.171, f32[4,4,64,128]{3,2,1,0:T(8,128)} %get-tuple-element.424, s32[]{:T(128)S(6)} %copy.39, f32[4,8,128]{2,1,0:T(8,128)S(1)} %bitcast.174, f32[4,128]{1,0:T(4,128)S(1)} %get-tuple-element.348, ...), kind=kOutput, calls=%fused_computation.76.clone.1 | convolution fusion | flops 406319104 | bytes 3315716 | tf_op jit(solution)/shard_map/while/body/eval_jaxpr/...fi,...fj->...ij/dot_general | solution.py:23
  137.6 1.2 scatter_custom_fusion
  138.9 0.6 gather_fusion.6
  139.5 1.2 scatter_custom_fusion.1
  140.7 18.8 %pmax.7 = f32[8,128]{1,0:T(8,128)S(1)} all-reduce(f32[8,128]{1,0:T(8,128)S(1)} %slice.26), channel_id=1, replica_groups=mesh['grp'=2,'src'=8,'tgt'=2] {'src'}, use_global_device_ids=true, to_apply=%region_11.12 | all-reduce | flops 1024 | bytes 8192 | tf_op jit(solution)/shard_map/pmax | solution.py:126
  159.5 17.5 %psum.7 = f32[8,128]{1,0:T(8,128)S(1)} all-reduce(f32[8,128]{1,0:T(8,128)S(1)} %slice_multiply_fusion), channel_id=1, replica_groups=mesh['grp'=2,'src'=8,'tgt'=2] {'src'}, use_global_device_ids=true, to_apply=%region_13.14 | all-reduce | flops 1024 | bytes 8192 | tf_op jit(solution)/shard_map/psum | solution.py:127
  (83 shorter events, 7.8 us)
Async XLA Ops:
  74.5 40.0 %copy-start = (s32[16,1]{0,1:T(1,128)S(1)}, s32[16,1]{0,1:T(1,128)}, u32[]{:S(2)}) copy-start(s32[16,1]{0,1:T(1,128)} %param.17) | copy-start | bytes 196
where the time goes:
time: 178 us
  blocking collectives  110 us (62%)
  matrix products  37.3 us (21%)
  local copies, waits for them, and re-layouts  19.9 us (11%)
  other arithmetic  9.29 us (5%)
    dot_general x8, matrix products, cost_tiles(): jnp.einsum('...fi,...fj->...ij', source_blk, target_blk, precision=lax.Pr...  37.3 us
    all_gather x1, blocking collectives, per_device(): lax.all_gather(target_feat, 'src', axis=0, tiled=True)  31 us
    all_gather x1, blocking collectives, per_device(): lax.all_gather(log_mass_tgt, 'src', axis=0, tiled=True)  22.4 us
    pmax x1, blocking collectives, per_device(): highest = lax.pmax(best, 'src')  18.8 us
    psum x1, blocking collectives, per_device(): whole = lax.psum(summed * jnp.exp(best - highest), 'src')  17.5 us
    all_gather x1, blocking collectives, per_device(): lax.all_gather(potential_tgt, 'src', axis=0, tiled=True)  16.5 us
    gather x8, local copies, waits for them, and re-layouts, row_pass(): return row_stats(cost, mass_all[ids_here], poten_all[ids_here], use_here)  4.59 us
    all_gather x2, blocking collectives, merged(): gathered = jax.tree.map(lambda a: lax.all_gather(a, axis), part)  3.63 us

commit v1 on v0

--- a/solution.py
+++ b/solution.py
@@ -124,7 +124,7 @@
     share = blocks // lax.axis_size("src")
     own_start = lax.axis_index("src") * share
     highest = lax.pmax(best, "src")
-    whole = lax.psum(summed * jnp.exp(best - highest), "src")
+    whole = jnp.sum(lax.all_gather(summed * jnp.exp(best - highest), "src"), axis=0)
     own_peak = lax.dynamic_slice_in_dim(highest, own_start, share, 0)
     own_total = lax.dynamic_slice_in_dim(whole, own_start, share, 0)
     potential_new = -entropic * (own_peak + jnp.log(own_total))

time: 178 us -> 191 us (1.073)
  blocking collectives: 110 us -> 123 us
    all_gather x0 -> x1, blocking collectives: none -> 30.6 us  [per_device(): lax.all_gather(summed * jnp.exp(best - highest), 'src')]
    psum x1 -> x0, blocking collectives: 17.5 us -> none  [per_device(): whole = lax.psum(summed * jnp.exp(best - highest), 'src')]
where the time goes in v1:
time: 191 us
  blocking collectives  123 us (64%)
  matrix products  37.3 us (20%)
  local copies, waits for them, and re-layouts  19.9 us (10%)
  other arithmetic  9.3 us (5%)
    dot_general x8, matrix products, cost_tiles(): jnp.einsum('...fi,...fj->...ij', source_blk, target_blk, precision=lax.Pr...  37.3 us
    all_gather x1, blocking collectives, per_device(): lax.all_gather(target_feat, 'src', axis=0, tiled=True)  31 us
    all_gather x1, blocking collectives, per_device(): lax.all_gather(summed * jnp.exp(best - highest), 'src')  30.6 us
    all_gather x1, blocking collectives, per_device(): lax.all_gather(log_mass_tgt, 'src', axis=0, tiled=True)  22.4 us
    pmax x1, blocking collectives, per_device(): highest = lax.pmax(best, 'src')  18.8 us
    all_gather x1, blocking collectives, per_device(): lax.all_gather(potential_tgt, 'src', axis=0, tiled=True)  16.5 us
    gather x8, local copies, waits for them, and re-layouts, row_pass(): return row_stats(cost, mass_all[ids_here], poten_all[ids_here], use_here)  4.59 us

profile of v1, /device:TPU:0, one launch (start us, length us, event | category | flops | bytes accessed | tf_op | source)
XLA Modules:
  0.0 190.7 jit_solution(6817240457990687223)
XLA Ops:
  1.2 1.3 reduce.3
  2.6 0.8 copy.19
  3.4 22.4 %all-gather.1 = f32[8,1,128]{2,1,0:T(1,128)S(1)} all-gather(f32[1,1,128]{2,1,0:T(1,128)} %bitcast.191), channel_id=1, replica_groups=mesh['grp'=2,'src'=8,'tgt'=2] {'src'}, dimensions={0}, use_global_device_ids=true | all-gather | bytes 4608 | tf_op jit(solution)/shard_map/all_gather | solution.py:70
  25.8 16.5 %all-gather.2 = f32[8,1,128]{2,1,0:T(1,128)S(1)} all-gather(f32[1,1,128]{2,1,0:T(1,128)} %bitcast.192), channel_id=1, replica_groups=mesh['grp'=2,'src'=8,'tgt'=2] {'src'}, dimensions={0}, use_global_device_ids=true | all-gather | bytes 4608 | tf_op jit(solution)/shard_map/all_gather | solution.py:71
  42.3 1.1 multiply_reduce_fusion
  43.4 31.0 %all_gather.23 = f32[8,64,128]{2,1,0:T(8,128)S(1)} all-gather(f32[1,64,128]{2,1,0:T(8,128)} %param.12), channel_id=1, replica_groups=mesh['grp'=2,'src'=8,'tgt'=2] {'src'}, dimensions={0}, use_global_device_ids=true | all-gather | bytes 294912 | tf_op jit(solution)/shard_map/all_gather | solution.py:69
  74.5 35.7 %while.8 = (s32[]{:T(128)}, f32[4,4,128]{2,1,0:T(4,128)S(1)}, f32[4,4,128]{2,1,0:T(4,128)S(1)}, pred[4,4,8]{2,1,0:T(4,128)(4,1)S(1)}, s32[4,4,8]{2,1,0:T(4,128)S...) while((s32[]{:T(128)}, f32[4,4,128]{2,1,0:T(4,128)S(1)}, ...), condition=%wide.region_5.6_spmd, body=%wide.region_2.5_spmd.sunk | while | flops 407896160 | bytes 7644529 | solution.py:94
  74.6 0.6 gather_fusion
  75.2 0.6 gather_fusion.1
  75.8 0.6 gather_fusion.2
  77.0 6.1 %fusion.44 = (f32[4,128]{1,0:T(4,128)S(1)}, f32[4,8,128,128]{2,3,1,0:T(8,128)S(1)}) fusion(f32[4,8,64,128]{3,2,1,0:T(8,128)S(1)} %bitcast.174, f32[4,4,64,128]{3,2,1,0:T(8,128)} %get-tuple-element.388, s32[]{:T(128)S(6)} %copy.30, f32[4,8,128]{2,1,0:T(8,128)S(1)} %bitcast.177, f32[4,128]{1,0:T(4,128)S(1)} %dynamic-slice_bitcast_fusion.9, ...), kind=kOutput, calls=%fused_computation.76.clone.1 | convolution fusion | flops 406846976 | bytes 3330084 | tf_op jit(solution)/shard_map/while/body/eval_jaxpr/...fi,...fj->...ij/dot_general | solution.py:23
  83.5 0.6 gather_fusion
  84.2 0.6 gather_fusion.1
  84.7 0.6 gather_fusion.2
  85.9 6.1 %fusion.44 = (f32[4,128]{1,0:T(4,128)S(1)}, f32[4,8,128,128]{2,3,1,0:T(8,128)S(1)}) fusion(f32[4,8,64,128]{3,2,1,0:T(8,128)S(1)} %bitcast.174, f32[4,4,64,128]{3,2,1,0:T(8,128)} %get-tuple-element.388, s32[]{:T(128)S(6)} %copy.30, f32[4,8,128]{2,1,0:T(8,128)S(1)} %bitcast.177, f32[4,128]{1,0:T(4,128)S(1)} %dynamic-slice_bitcast_fusion.9, ...), kind=kOutput, calls=%fused_computation.76.clone.1 | convolution fusion | flops 406846976 | bytes 3330084 | tf_op jit(solution)/shard_map/while/body/eval_jaxpr/...fi,...fj->...ij/dot_general | solution.py:23
  92.5 0.6 gather_fusion
  93.1 0.6 gather_fusion.1
  93.7 0.6 gather_fusion.2
  94.8 6.1 %fusion.44 = (f32[4,128]{1,0:T(4,128)S(1)}, f32[4,8,128,128]{2,3,1,0:T(8,128)S(1)}) fusion(f32[4,8,64,128]{3,2,1,0:T(8,128)S(1)} %bitcast.174, f32[4,4,64,128]{3,2,1,0:T(8,128)} %get-tuple-element.388, s32[]{:T(128)S(6)} %copy.30, f32[4,8,128]{2,1,0:T(8,128)S(1)} %bitcast.177, f32[4,128]{1,0:T(4,128)S(1)} %dynamic-slice_bitcast_fusion.9, ...), kind=kOutput, calls=%fused_computation.76.clone.1 | convolution fusion | flops 406846976 | bytes 3330084 | tf_op jit(solution)/shard_map/while/body/eval_jaxpr/...fi,...fj->...ij/dot_general | solution.py:23
  101.4 0.6 gather_fusion
  102.0 0.6 gather_fusion.1
  102.6 0.6 gather_fusion.2
  103.8 6.1 %fusion.44 = (f32[4,128]{1,0:T(4,128)S(1)}, f32[4,8,128,128]{2,3,1,0:T(8,128)S(1)}) fusion(f32[4,8,64,128]{3,2,1,0:T(8,128)S(1)} %bitcast.174, f32[4,4,64,128]{3,2,1,0:T(8,128)} %get-tuple-element.388, s32[]{:T(128)S(6)} %copy.30, f32[4,8,128]{2,1,0:T(8,128)S(1)} %bitcast.177, f32[4,128]{1,0:T(4,128)S(1)} %dynamic-slice_bitcast_fusion.9, ...), kind=kOutput, calls=%fused_computation.76.clone.1 | convolution fusion | flops 406846976 | bytes 3330084 | tf_op jit(solution)/shard_map/while/body/eval_jaxpr/...fi,...fj->...ij/dot_general | solution.py:23
  110.2 1.8 all_gather.25
  112.0 1.8 all_gather.24
  113.9 0.6 fusion.19
  114.8 22.8 %while.9 = (s32[]{:T(128)}, f32[4,4,8,128]{3,2,1,0:T(8,128)S(1)}, f32[4,4,8,128]{3,2,1,0:T(8,128)S(1)}, pred[4,4,8]{2,1,0:T(4,128)(4,1)S(1)}, f32[4,4,128]{2,1,0...) while((s32[]{:T(128)}, f32[4,4,8,128]{3,2,1,0:T(8,128)S(1)}, ...), condition=%wide.region_9.10_spmd, body=%wide.region_6.9_spmd.sunk | while | flops 407372896 | bytes 7659093 | solution.py:109
  114.9 0.6 gather_fusion.4
  115.6 0.6 gather_fusion.5
  116.2 0.7 dynamic-slice_bitcast_fusion.12
  116.9 3.2 %fusion.46 = (f32[4,8,128]{2,1,0:T(8,128)S(1)}, f32[4,8,128,128]{3,2,1,0:T(8,128)S(1)}) fusion(f32[4,8,64,128]{3,2,1,0:T(8,128)S(1)} %bitcast.173, f32[4,4,64,128]{3,2,1,0:T(8,128)} %get-tuple-element.424, s32[]{:T(128)S(6)} %copy.39, f32[4,8,128]{2,1,0:T(8,128)S(1)} %bitcast.176, f32[4,128]{1,0:T(4,128)S(1)} %get-tuple-element.348, ...), kind=kOutput, calls=%fused_computation.77.clone.1 | convolution fusion | flops 406319104 | bytes 3315716 | tf_op jit(solution)/shard_map/while/body/eval_jaxpr/...fi,...fj->...ij/dot_general | solution.py:23
  120.6 0.6 gather_fusion.4
  121.3 0.6 gather_fusion.5
  121.9 0.7 dynamic-slice_bitcast_fusion.12
  122.5 3.2 %fusion.46 = (f32[4,8,128]{2,1,0:T(8,128)S(1)}, f32[4,8,128,128]{3,2,1,0:T(8,128)S(1)}) fusion(f32[4,8,64,128]{3,2,1,0:T(8,128)S(1)} %bitcast.173, f32[4,4,64,128]{3,2,1,0:T(8,128)} %get-tuple-element.424, s32[]{:T(128)S(6)} %copy.39, f32[4,8,128]{2,1,0:T(8,128)S(1)} %bitcast.176, f32[4,128]{1,0:T(4,128)S(1)} %get-tuple-element.348, ...), kind=kOutput, calls=%fused_computation.77.clone.1 | convolution fusion | flops 406319104 | bytes 3315716 | tf_op jit(solution)/shard_map/while/body/eval_jaxpr/...fi,...fj->...ij/dot_general | solution.py:23
  126.3 0.6 gather_fusion.4
  127.0 0.6 gather_fusion.5
  127.6 0.7 dynamic-slice_bitcast_fusion.12
  128.2 3.2 %fusion.46 = (f32[4,8,128]{2,1,0:T(8,128)S(1)}, f32[4,8,128,128]{3,2,1,0:T(8,128)S(1)}) fusion(f32[4,8,64,128]{3,2,1,0:T(8,128)S(1)} %bitcast.173, f32[4,4,64,128]{3,2,1,0:T(8,128)} %get-tuple-element.424, s32[]{:T(128)S(6)} %copy.39, f32[4,8,128]{2,1,0:T(8,128)S(1)} %bitcast.176, f32[4,128]{1,0:T(4,128)S(1)} %get-tuple-element.348, ...), kind=kOutput, calls=%fused_computation.77.clone.1 | convolution fusion | flops 406319104 | bytes 3315716 | tf_op jit(solution)/shard_map/while/body/eval_jaxpr/...fi,...fj->...ij/dot_general | solution.py:23
  132.0 0.6 gather_fusion.4
  132.7 0.6 gather_fusion.5
  133.3 0.7 dynamic-slice_bitcast_fusion.12
  133.9 3.2 %fusion.46 = (f32[4,8,128]{2,1,0:T(8,128)S(1)}, f32[4,8,128,128]{3,2,1,0:T(8,128)S(1)}) fusion(f32[4,8,64,128]{3,2,1,0:T(8,128)S(1)} %bitcast.173, f32[4,4,64,128]{3,2,1,0:T(8,128)} %get-tuple-element.424, s32[]{:T(128)S(6)} %copy.39, f32[4,8,128]{2,1,0:T(8,128)S(1)} %bitcast.176, f32[4,128]{1,0:T(4,128)S(1)} %get-tuple-element.348, ...), kind=kOutput, calls=%fused_computation.77.clone.1 | convolution fusion | flops 406319104 | bytes 3315716 | tf_op jit(solution)/shard_map/while/body/eval_jaxpr/...fi,...fj->...ij/dot_general | solution.py:23
  137.6 1.2 scatter_custom_fusion
  138.9 0.6 gather_fusion.6
  139.5 1.2 scatter_custom_fusion.1
  140.7 18.8 %pmax.7 = f32[8,128]{1,0:T(8,128)S(1)} all-reduce(f32[8,128]{1,0:T(8,128)S(1)} %slice.26), channel_id=1, replica_groups=mesh['grp'=2,'src'=8,'tgt'=2] {'src'}, use_global_device_ids=true, to_apply=%region_11.12 | all-reduce | flops 1024 | bytes 8192 | tf_op jit(solution)/shard_map/pmax | solution.py:126
  159.5 30.6 %all-gather = f32[64,128]{1,0:T(8,128)S(1)} all-gather(f32[8,128]{1,0:T(8,128)S(1)} %slice_multiply_fusion), channel_id=2, replica_groups=mesh['grp'=2,'src'=8,'tgt'=2] {'src'}, dimensions={0}, use_global_device_ids=true | all-gather | bytes 36864 | tf_op jit(solution)/shard_map/all_gather | solution.py:127
  (84 shorter events, 7.8 us)
Async XLA Ops:
  74.5 40.0 %copy-start = (s32[16,1]{0,1:T(1,128)S(1)}, s32[16,1]{0,1:T(1,128)}, u32[]{:S(2)}) copy-start(s32[16,1]{0,1:T(1,128)} %param.17) | copy-start | bytes 196
